TPU v7x, 256 devices: a whole 4x4x8 slice. The times are simulated.
256 devices in a mesh: trow: 16 (over x, y), tcol: 8 (over z), rep: 2 (over core).
Axes of the slice: x: 4, y: 4, z: 8, core: 2. Of those that a mesh axis runs over, the one named last changes fastest.
Arguments:
- users: float32 [131072, 128], P(('trow', 'tcol'))
- items: float32 [65536, 128], P(('tcol', 'trow'))
- ratings: bfloat16 [16, 8, 2, 64, 128, 128], P('trow', 'tcol', 'rep'), may hold values from -6 to 6
- row_mask: int32 [16, 8, 2, 64, 128], P('trow', 'tcol', 'rep'), may hold values 0 or 1
- col_mask: int32 [16, 8, 2, 64, 128], P('trow', 'tcol', 'rep'), may hold values 0 or 1
- row_slots: int32 [16, 8, 2, 64], P('trow', 'tcol', 'rep'), may hold values from 0 to 31, as said below
- col_slots: int32 [16, 8, 2, 64], P('trow', 'tcol', 'rep'), may hold values from 0 to 31, as said below
- send_users: int32 [16, 8, 2, 8, 4], P('trow', 'tcol', 'rep'), may hold values from 0 to 7, as said below
- send_items: int32 [16, 8, 2, 16, 2], P('trow', 'tcol', 'rep'), may hold values from 0 to 3, as said below
Outputs:
- users_out: float32 [131072, 128], P(('trow', 'tcol'))
- items_out: float32 [65536, 128], P(('tcol', 'trow'))
Inputs may be any that keep to these rules, and one draw needn't show every extreme that they name: `send_users`: distinct within each row of the last dimension. `send_items`: distinct within each row of the last dimension. `row_slots`: every slot is named by some tile of each device. `col_slots`: every slot is named by some tile of each device.
All inputs are finite; a program needn't handle non-finite values. No bound on the sum of `row_mask` or of `col_mask` on one device may be relied on, other than what follows from the above.
Results may differ from a plain program's by a relative error of at most 0.02.
Values may be sent and summed in bfloat16 or wider, within the bound.
A program may use at most 64 MiB of HBM per device.

v0:
```python
import jax
import jax.numpy as jnp
from jax import lax
from jax.sharding import PartitionSpec as P

ITERS = 2


def precondition(gradient, gramian):
    factor = jnp.linalg.cholesky(gramian)
    return jax.scipy.linalg.cho_solve((factor, True), gradient.T).T


def pool_sum(index_list, terms, pool_count):
    onehot = (
        lax.broadcasted_iota(jnp.int32, (pool_count, index_list.shape[0]), 0) == index_list[None, :]
    ).astype(jnp.bfloat16)
    flat = terms.reshape(terms.shape[0], -1)
    upper = flat.astype(jnp.bfloat16)
    lower = (flat - upper.astype(jnp.float32)).astype(jnp.bfloat16)
    return jnp.dot(onehot, upper, preferred_element_type=jnp.float32) + jnp.dot(
        onehot, lower, preferred_element_type=jnp.float32
    )


def on_device(
    users, items, ratings, row_mask, col_mask, row_slots, col_slots, send_users, send_items
):
    n_trow = lax.axis_size("trow")
    n_tcol = lax.axis_size("tcol")
    n_rep = lax.axis_size("rep")
    tile_size = ratings.shape[-1]
    rank_width = users.shape[1]
    tile_count = ratings.shape[3]
    own_users = users.shape[0] // tile_size
    own_items = items.shape[0] // tile_size
    user_cap = send_users.shape[-1]
    item_cap = send_items.shape[-1]
    ratings_local = ratings.reshape(tile_count, tile_size, tile_size)
    weights = (
        row_mask.reshape(tile_count, tile_size)[:, :, None]
        * col_mask.reshape(tile_count, tile_size)[:, None, :]
    ).astype(jnp.float32)
    row_slot_list = row_slots.reshape(-1)
    col_slot_list = col_slots.reshape(-1)
    user_sends = send_users.reshape(n_tcol, -1)
    item_sends = send_items.reshape(n_trow, -1)
    user_received = lax.all_to_all(
        user_sends, "tcol", split_axis=0, concat_axis=0, tiled=True
    ).reshape(-1)
    item_received = lax.all_to_all(
        item_sends, "trow", split_axis=0, concat_axis=0, tiled=True
    ).reshape(-1)
    row_list = row_slot_list // user_cap * own_users + user_received[row_slot_list]
    col_list = col_slot_list // item_cap * own_items + item_received[col_slot_list]
    all_users = own_users * tile_size * n_trow * n_tcol
    all_items = own_items * tile_size * n_trow * n_tcol
    user_coef = 2.0 * all_items * own_users / (tile_size * tile_count * n_rep)
    item_coef = 2.0 * all_users * own_items / (tile_size * tile_count * n_rep)
    for iteration in range(ITERS):
        gram_users, gram_items = lax.psum(
            (
                jnp.dot(
                    users.T,
                    users,
                    precision=lax.Precision.HIGHEST,
                    preferred_element_type=jnp.float32,
                ),
                jnp.dot(
                    items.T,
                    items,
                    precision=lax.Precision.HIGHEST,
                    preferred_element_type=jnp.float32,
                ),
            ),
            ("trow", "tcol"),
        )
        user_half = users.astype(jnp.bfloat16).reshape(own_users, tile_size, rank_width)
        item_half = items.astype(jnp.bfloat16).reshape(own_items, tile_size, rank_width)
        user_pool = lax.all_gather(user_half, "tcol", axis=0, tiled=True)
        item_pool = lax.all_gather(item_half, "trow", axis=0, tiled=True)
        x_tiles = user_pool[row_list]
        y_tiles = item_pool[col_list]
        predicted = jnp.einsum("tar,tbr->tab", x_tiles, y_tiles, preferred_element_type=jnp.float32)
        errors = (weights * (predicted - ratings_local.astype(jnp.float32))).astype(jnp.bfloat16)
        user_terms = jnp.einsum("tab,tbr->tar", errors, y_tiles, preferred_element_type=jnp.float32)
        item_terms = jnp.einsum("tab,tar->tbr", errors, x_tiles, preferred_element_type=jnp.float32)
        user_pooled = pool_sum(row_list, user_terms, user_pool.shape[0])
        item_pooled = pool_sum(col_list, item_terms, item_pool.shape[0])
        user_grad = lax.psum_scatter(user_pooled, "tcol", scatter_dimension=0, tiled=True)
        item_grad = lax.psum_scatter(item_pooled, "trow", scatter_dimension=0, tiled=True)
        user_grad, item_grad = lax.psum((user_grad, item_grad), "rep")
        new_users = users - user_coef * precondition(user_grad.reshape(-1, rank_width), gram_items)
        new_items = items - item_coef * precondition(item_grad.reshape(-1, rank_width), gram_users)
        users, items = (new_users, new_items)
    return (users, items)


def solution(mesh):
    return jax.shard_map(
        on_device,
        mesh=mesh,
        in_specs=(
            P(("trow", "tcol"), None),
            P(("tcol", "trow"), None),
            P("trow", "tcol", "rep", None, None, None),
            P("trow", "tcol", "rep", None, None),
            P("trow", "tcol", "rep", None, None),
            P("trow", "tcol", "rep", None),
            P("trow", "tcol", "rep", None),
            P("trow", "tcol", "rep", None, None),
            P("trow", "tcol", "rep", None, None),
        ),
        out_specs=(P(("trow", "tcol"), None), P(("tcol", "trow"), None)),
        check_vma=False,
    )
```

profile of v0, /device:TPU:1, one launch (start us, length us, event | category | flops | bytes accessed | tf_op | source)
XLA Modules:
  0.0 1075.5 jit_solution(2654260133140196737)
XLA Ops:
  7.2 1.8 convert_element_type.69
  9.1 1.6 convert_element_type.70
  10.7 1.3 copy.48
  12.1 7.6 all-to-all-start.1
  21.0 1.3 copy.47
  22.3 3.7 all-to-all-done.1
  26.1 8.2 all-to-all-start
  36.4 4.4 all-to-all-done
  42.3 9.4 all-gather.5.cloned.1.call-done
  51.7 3.7 gather_fusion.1
  55.4 50.8 %all-gather.7.cloned.1.call-done = bf16[64,128,128]{2,1,0:T(8,128)(2,1)} async-done(((bf16[4,128,128]{2,1,0:T(8,128)(2,1)}), bf16[64,128,128]{2,1,0:T(8,128)(2,1)}) %all-gather.7.cloned.1.call-update) | async-done | bytes 2097168 | tf_op jit(solution)/shard_map/all_gather | solution.py:81
  106.3 2.5 gather_fusion.3
  108.9 4.1 fusion.1
  113.0 0.9 fusion.61
  114.4 2.8 fusion.9
  117.2 4.9 convolution_add_fusion.2
  122.3 2.3 fusion.59
  124.6 2.8 fusion.8
  127.4 4.9 convolution_add_fusion.3
  132.4 0.9 copy-done.5
  133.2 1.2 fusion.58
  134.5 1.6 fusion.60
  137.4 98.5 %all-reduce.13.cloned.1.call-done = f32[64,16384]{1,0:T(8,128)} async-done(((f32[64,16384]{1,0:T(8,128)}), f32[64,16384]{1,0:T(8,128)}) %all-reduce.13.cloned.1.call-update) | async-done | bytes 4194320
  235.9 1.1 constant_dynamic-slice_fusion.1
  237.0 0.9 reshape.383
  237.9 55.8 %reduce-scatter.3.cloned.1.call-done = f32[8,16384]{1,0:T(8,128)} async-done(((f32[64,16384]{1,0:T(8,128)}), f32[8,16384]{1,0:T(8,128)}) %reduce-scatter.3.cloned.1.call-update) | async-done | bytes 524304 | tf_op jit(solution)/shard_map/reduce_scatter | solution.py:90
  293.7 1.9 reshape.380
  296.1 209.1 %all-reduce.19.cloned.1.call-done = (f32[128,128]{0,1:T(8,128)}, f32[128,128]{0,1:T(8,128)}) async-done(((f32[128,128]{0,1:T(8,128)}, f32[128,128]{0,1:T(8,128)}), (f32[128,128]{0,1:T(8,128)}, f32[128,128]{0,1:T(8,128)})) %all-reduce.19.cloned.1.call-update) | async-done | bytes 131088 | tf_op jit(solution)/shard_map/psum | solution.py:61
  505.3 0.9 copy.51
  506.2 0.9 copy.46
  507.1 0.9 fusion.39
  508.0 11.7 %cholesky.74 = f32[128,128]{1,0:T(8,128)S(1)} custom-call(f32[128,128]{1,0:T(8,128)S(1)} %get-tuple-element.24), custom_call_target="Cholesky" | custom-call | tf_op jit(solution)/shard_map/jit(cholesky)/cholesky | solution.py:10
  521.1 9.8 custom-call.14
  530.9 10.3 all-reduce.23.cloned.1.call-done
  541.2 1.7 fusion.41
  545.1 11.7 %cholesky.85 = f32[128,128]{1,0:T(8,128)S(1)} custom-call(f32[128,128]{1,0:T(8,128)S(1)} %get-tuple-element.23), custom_call_target="Cholesky" | custom-call | tf_op jit(solution)/shard_map/jit(cholesky)/cholesky | solution.py:10
  558.1 9.8 custom-call.15
  569.6 1.0 fusion.62
  570.6 1.2 fusion.64
  572.0 10.9 %all-gather.9.cloned.1.call-done = bf16[64,128,128]{2,1,0:T(8,128)(2,1)} async-done(((bf16[8,128,128]{2,1,0:T(8,128)(2,1)}), bf16[64,128,128]{2,1,0:T(8,128)(2,1)}) %all-gather.9.cloned.1.call-update) | async-done | bytes 2097168 | tf_op jit(solution)/shard_map/all_gather | solution.py:80
  582.9 3.7 gather_fusion.4
  586.7 50.5 %all-gather.11.cloned.1.call-done = bf16[64,128,128]{2,1,0:T(8,128)(2,1)} async-done(((bf16[4,128,128]{2,1,0:T(8,128)(2,1)}), bf16[64,128,128]{2,1,0:T(8,128)(2,1)}) %all-gather.11.cloned.1.call-update) | async-done | bytes 2097168 | tf_op jit(solution)/shard_map/all_gather | solution.py:81
  637.2 2.5 gather_fusion.5
  639.7 4.1 fusion.3
  643.9 0.9 fusion.65
  645.2 2.8 fusion.11
  648.0 4.9 convolution_add_fusion
  653.0 2.3 fusion.63
  655.3 2.8 fusion.10
  658.1 4.9 convolution_add_fusion.1
  663.2 187.3 %all-reduce.17.cloned.1.call-done = (f32[128,128]{0,1:T(8,128)}, f32[128,128]{0,1:T(8,128)}) async-done(((f32[128,128]{0,1:T(8,128)}, f32[128,128]{0,1:T(8,128)}), (f32[128,128]{0,1:T(8,128)}, f32[128,128]{0,1:T(8,128)})) %all-reduce.17.cloned.1.call-update) | async-done | bytes 131088 | tf_op jit(solution)/shard_map/psum | solution.py:61
  850.6 1.0 copy.55
  851.5 0.9 fusion.35
  852.4 11.7 %cholesky.96 = f32[128,128]{1,0:T(8,128)S(1)} custom-call(f32[128,128]{1,0:T(8,128)S(1)} %fusion.35), custom_call_target="Cholesky" | custom-call | tf_op jit(solution)/shard_map/jit(cholesky)/cholesky | solution.py:10
  864.8 104.5 %all-reduce.15.cloned.1.call-done = f32[64,16384]{1,0:T(8,128)} async-done(((f32[64,16384]{1,0:T(8,128)}), f32[64,16384]{1,0:T(8,128)}) %all-reduce.15.cloned.1.call-update) | async-done | bytes 4194320
  969.4 1.1 constant_dynamic-slice_fusion
  970.5 0.9 reshape.389
  971.4 56.1 %reduce-scatter.5.cloned.1.call-done = f32[8,16384]{1,0:T(8,128)} async-done(((f32[64,16384]{1,0:T(8,128)}), f32[8,16384]{1,0:T(8,128)}) %reduce-scatter.5.cloned.1.call-update) | async-done | bytes 524304 | tf_op jit(solution)/shard_map/reduce_scatter | solution.py:90
  1027.5 1.9 reshape.387
  1030.1 9.8 custom-call.16
  1040.0 11.7 %cholesky.107 = f32[128,128]{1,0:T(8,128)S(1)} custom-call(f32[128,128]{1,0:T(8,128)S(1)} %fusion.31), custom_call_target="Cholesky" | custom-call | tf_op jit(solution)/shard_map/jit(cholesky)/cholesky | solution.py:10
  1053.2 10.0 custom-call.17
  1063.3 1.7 fusion.33
  1065.6 1.0 copy.61
  (95 shorter events, 19.6 us)
Async XLA Ops:
  7.2 35.1 %copy-start.12 = (s32[1,1,1,64]{3,2,1,0:T(1,128)S(1)}, s32[1,1,1,64]{3,2,1,0:T(1,128)}, u32[]{:S(2)}) copy-start(s32[1,1,1,64]{3,2,1,0:T(1,128)} %param.19) | copy-start | bytes 772
  7.2 29.1 %copy-start.11 = (s32[1,1,1,64]{3,2,1,0:T(1,128)S(1)}, s32[1,1,1,64]{3,2,1,0:T(1,128)}, u32[]{:S(2)}) copy-start(s32[1,1,1,64]{3,2,1,0:T(1,128)} %param.20) | copy-start | bytes 772
  7.2 44.5 %all-gather.5.cloned.1.call-start = ((), (), s32[]{:S(2)}) async-start(), calls=%async_computation.4 | async-start | bytes 2359296 | tf_op jit(solution)/shard_map/all_gather | solution.py:80
  9.0 97.3 %all-gather.7.cloned.1.call-start = ((), (), s32[]{:S(2)}) async-start(), calls=%async_computation.5 | async-start | bytes 2228224 | tf_op jit(solution)/shard_map/all_gather | solution.py:81
  12.1 14.0 %all-to-all-start.1 = ((s32[16,1,2]{2,1,0:T(1,128)}), s32[16,1,2]{2,1,0:T(1,128)S(1)}, u32[]{:S(2)}, u32[]{:S(2)}) async-start(s32[16,1,2]{2,1,0:T(1,128)} %copy.48), calls=%async_computation.1 | async-start | bytes 16384 | tf_op jit(solution)/shard_map/all_to_all | solution.py:51
  26.1 14.7 %all-to-all-start = ((s32[8,1,4]{2,1,0:T(1,128)}), s32[8,1,4]{2,1,0:T(1,128)S(1)}, u32[]{:S(2)}, u32[]{:S(2)}) async-start(s32[8,1,4]{2,1,0:T(1,128)} %copy.47), calls=%async_computation | async-start | bytes 8192 | tf_op jit(solution)/shard_map/all_to_all | solution.py:48
  34.3 201.6 %all-reduce.13.cloned.1.call-start = ((), (), s32[]{:S(2)}) async-start(), calls=%async_computation.10 | async-start | bytes 8388608
  55.4 53.4 %copy-start.9 = (s32[1,1,1,64,128]{4,3,2,1,0:T(8,128)S(1)}, s32[1,1,1,64,128]{4,3,2,1,0:T(8,128)}, u32[]{:S(2)}) copy-start(s32[1,1,1,64,128]{4,3,2,1,0:T(8,128)} %param.18) | copy-start | bytes 98308
  55.4 53.4 %copy-start.10 = (s32[1,1,1,64,128]{4,3,2,1,0:T(8,128)S(1)}, s32[1,1,1,64,128]{4,3,2,1,0:T(8,128)}, u32[]{:S(2)}) copy-start(s32[1,1,1,64,128]{4,3,2,1,0:T(8,128)} %param.17) | copy-start | bytes 98308
  108.9 4.1 copy-start.1
  113.0 1.4 copy-start.2
  122.1 171.6 %reduce-scatter.3.cloned.1.call-start = ((), (), s32[]{:S(2)}) async-start(), calls=%async_computation.6 | async-start | bytes 4718592 | tf_op jit(solution)/shard_map/reduce_scatter | solution.py:90
  132.3 1.0 copy-start.5
  132.3 2.2 copy-start.4
  132.3 3.9 copy-start.13
  132.3 372.9 %all-reduce.19.cloned.1.call-start = ((), (), s32[]{:S(2)}) async-start(), calls=%async_computation.13 | async-start | bytes 262144 | tf_op jit(solution)/shard_map/psum | solution.py:61
  136.1 405.1 %all-reduce.23.cloned.1.call-start = ((), (), s32[]{:S(2)}) async-start(), calls=%async_computation.15 | async-start | bytes 1572864 | tf_op jit(solution)/shard_map/psum | solution.py:92
  295.6 287.3 %all-gather.9.cloned.1.call-start = ((), (), s32[]{:S(2)}) async-start(), calls=%async_computation.7 | async-start | bytes 2359296 | tf_op jit(solution)/shard_map/all_gather | solution.py:80
  541.2 26.7 %copy-start.7 = (f32[128,512]{0,1:T(8,128)S(1)}, f32[128,512]{0,1:T(8,128)}, u32[]{:S(2)}) copy-start(f32[128,512]{0,1:T(8,128)} %get-tuple-element.18) | copy-start | bytes 786436
  544.4 92.8 %all-gather.11.cloned.1.call-start = ((), (), s32[]{:S(2)}) async-start(), calls=%async_computation.8 | async-start | bytes 2228224 | tf_op jit(solution)/shard_map/all_gather | solution.py:81
  569.5 281.0 %all-reduce.17.cloned.1.call-start = ((), (), s32[]{:S(2)}) async-start(), calls=%async_computation.12 | async-start | bytes 262144 | tf_op jit(solution)/shard_map/psum | solution.py:61
  571.8 397.6 %all-reduce.15.cloned.1.call-start = ((), (), s32[]{:S(2)}) async-start(), calls=%async_computation.11 | async-start | bytes 8388608
  639.7 4.1 copy-start
  643.9 1.4 copy-start.3
  652.9 374.5 %reduce-scatter.5.cloned.1.call-start = ((), (), s32[]{:S(2)}) async-start(), calls=%async_computation.9 | async-start | bytes 4718592 | tf_op jit(solution)/shard_map/reduce_scatter | solution.py:90
  663.0 400.3 %all-reduce.21.cloned.1.call-start = ((), (), s32[]{:S(2)}) async-start(), calls=%async_computation.14 | async-start | bytes 1572864 | tf_op jit(solution)/shard_map/psum | solution.py:92
  850.6 189.4 %copy-start.6 = (f32[128,128]{0,1:T(8,128)S(1)}, f32[128,128]{0,1:T(8,128)}, u32[]{:S(2)}) copy-start(f32[128,128]{0,1:T(8,128)} %get-tuple-element.12) | copy-start | bytes 196612
  1063.2 3.3 copy-start.8
Sparse Core Ops, SparseCore 0:
  10.4 41.2 all-gather.4
  54.7 51.5 all-gather.6
  122.2 113.6 all-reduce.12
  238.3 55.3 reduce-scatter.2
  299.1 206.1 all-reduce.18
  508.5 32.6 all-reduce.22
  544.5 38.3 all-gather.8
  585.9 51.1 all-gather.10
  642.7 207.7 all-reduce.16
  854.1 115.2 all-reduce.14
  972.1 55.3 reduce-scatter.4
  1030.7 29.7 all-reduce.20
where the time goes:
time: 1080 us
  waiting for transfers between devices  852 us (79%)
  other arithmetic  99.6 us (9%)
  matrix products  56.4 us (5%)
  local copies, waits for them, and re-layouts  34.4 us (3%)
  starting transfers between devices  17.6 us (2%)
  between operations  15.7 us (1%)
    psum x2, waiting for transfers between devices, on_device(): lax.psum((jnp.dot(users.T, users, precision=lax.Precision.HIGHEST, prefer...  396 us
    unnamed x14, waiting for transfers between devices  203 us
    reduce_scatter x2, waiting for transfers between devices, on_device(): lax.psum_scatter(user_pooled, 'tcol', scatter_dimension=0, tiled=True)  112 us
    all_gather x2, waiting for transfers between devices, on_device(): item_pool = lax.all_gather(item_half, 'trow', axis=0, tiled=True)  101 us
    another operation x12, other arithmetic, precondition(): factor = jnp.linalg.cholesky(gramian)  49.7 us
    another operation x8, other arithmetic, precondition(): return jax.scipy.linalg.cho_solve((factor, True), gradient.T).T  42.1 us
  transfers between devices with their start and end apart: 14, of which 13 were waited for; matrix products, arithmetic and copies ran while one was open for 15% of the time, Pallas kernels for 0%

commit v1 on v0

--- a/solution.py
+++ b/solution.py
@@ -4,6 +4,24 @@
 from jax.sharding import PartitionSpec as P
 
 ITERS = 2
+
+
+def gather_around(array, axis, dim):
+    ways, here, lap = (lax.axis_size(axis), lax.axis_index(axis), array.shape[dim])
+    lengths = [n * ways if d == dim else n for d, n in enumerate(array.shape)]
+    full = lax.dynamic_update_slice_in_dim(
+        jnp.zeros(lengths, array.dtype), array, here * lap, axis=dim
+    )
+    going_up = going_down = array
+    for far in range(1, ways // 2 + 1):
+        going_up = lax.ppermute(going_up, axis, [(d, (d + 1) % ways) for d in range(ways)])
+        full = lax.dynamic_update_slice_in_dim(full, going_up, (here - far) % ways * lap, axis=dim)
+        if 2 * far < ways:
+            going_down = lax.ppermute(going_down, axis, [(d, (d - 1) % ways) for d in range(ways)])
+            full = lax.dynamic_update_slice_in_dim(
+                full, going_down, (here + far) % ways * lap, axis=dim
+            )
+    return full
 
 
 def precondition(gradient, gramian):
@@ -78,7 +96,7 @@
         user_half = users.astype(jnp.bfloat16).reshape(own_users, tile_size, rank_width)
         item_half = items.astype(jnp.bfloat16).reshape(own_items, tile_size, rank_width)
         user_pool = lax.all_gather(user_half, "tcol", axis=0, tiled=True)
-        item_pool = lax.all_gather(item_half, "trow", axis=0, tiled=True)
+        item_pool = gather_around(item_half, "trow", 0)
         x_tiles = user_pool[row_list]
         y_tiles = item_pool[col_list]
         predicted = jnp.einsum("tar,tbr->tab", x_tiles, y_tiles, preferred_element_type=jnp.float32)

time: 1080 us -> 1030 us (0.954)
  waiting for transfers between devices: 852 us -> 706 us
  starting transfers between devices: 17.6 us -> 83.7 us
  local copies, waits for them, and re-layouts: 34.4 us -> 58.6 us
    all_gather x2 -> x0, waiting for transfers between devices: 101 us -> none  [on_device(): item_pool = lax.all_gather(item_half, 'trow', axis=0, tiled=True)]
    ppermute x0 -> x30, starting transfers between devices: none -> 70.3 us  [the longest x14 66.4 us: gather_around(): lax.ppermute(going_down, axis, [(d, (d - 1) % ways) for d in range(ways)])]
    psum x2, waiting for transfers between devices: 396 us -> 347 us  [on_device(): lax.psum((jnp.dot(users.T, users, precision=lax.Precision.HIGHEST, prefer...]
    ppermute x0 -> x30, waiting for transfers between devices: none -> 25.5 us  [the longest x16 25.5 us: gather_around(): lax.ppermute(going_up, axis, [(d, (d + 1) % ways) for d in range(ways)])]
    dynamic_update_slice x0 -> x32, local copies, waits for them, and re-layouts: none -> 21.1 us  [the longest x16 10.6 us: gather_around(): lax.dynamic_update_slice_in_dim(full, going_up, (here - far) % ways * lap...]
    all_gather x2, waiting for transfers between devices: 20.3 us -> 0.04 us  [on_device(): user_pool = lax.all_gather(user_half, 'tcol', axis=0, tiled=True)]
    unnamed x14 -> x12, waiting for transfers between devices: 203 us -> 206 us
  transfers between devices with their start and end apart: 14 -> 42, of which waited for: 13 -> 23; matrix products, arithmetic and copies ran while one was open for 15% -> 18% of each run, Pallas kernels for 0% -> 0%
where the time goes in v1:
time: 1030 us; the launch traced here: 1020 us
  waiting for transfers between devices  706 us (69%)
  other arithmetic  98.7 us (10%)
  starting transfers between devices  83.7 us (8%)
  local copies, waits for them, and re-layouts  58.6 us (6%)
  matrix products  56.5 us (5%)
  between operations  15.8 us (2%)
    psum x2, waiting for transfers between devices, on_device(): lax.psum((jnp.dot(users.T, users, precision=lax.Precision.HIGHEST, prefer...  347 us
    unnamed x12, waiting for transfers between devices  206 us
    reduce_scatter x2, waiting for transfers between devices, on_device(): lax.psum_scatter(user_pooled, 'tcol', scatter_dimension=0, tiled=True)  112 us
    ppermute x14, starting transfers between devices, gather_around(): lax.ppermute(going_down, axis, [(d, (d - 1) % ways) for d in range(ways)])  66.4 us
    another operation x12, other arithmetic, precondition(): factor = jnp.linalg.cholesky(gramian)  49.6 us
    another operation x8, other arithmetic, precondition(): return jax.scipy.linalg.cho_solve((factor, True), gradient.T).T  42 us
    ppermute x16, waiting for transfers between devices, gather_around(): lax.ppermute(going_up, axis, [(d, (d + 1) % ways) for d in range(ways)])  25.5 us
  transfers between devices with their start and end apart: 42, of which 23 were waited for; matrix products, arithmetic and copies ran while one was open for 18% of the time, Pallas kernels for 0%

profile of v1, /device:TPU:1, one launch (start us, length us, event | category | flops | bytes accessed | tf_op | source)
XLA Modules:
  0.0 1019.6 jit_solution(9080624345771083262)
XLA Ops:
  7.2 1.8 convert_element_type.69
  10.0 2.2 collective-permute-start
  12.2 3.7 collective-permute-start.1
  15.9 1.4 copy.66
  17.3 3.5 all-to-all-start.1
  21.0 1.3 copy.65
  23.7 1.8 broadcast.338.clone
  27.0 8.2 all-to-all-start
  37.4 4.5 all-to-all-done
  43.7 4.6 collective-permute-start.3
  50.6 4.8 collective-permute-start.5
  57.8 4.8 collective-permute-start.7
  64.9 4.8 collective-permute-start.9
  71.0 1.9 collective-permute-done.8
  72.9 5.1 collective-permute-start.11
  79.4 1.7 collective-permute-done.10
  81.1 5.1 collective-permute-start.13
  89.6 5.8 collective-permute-done.14
  96.1 2.5 gather_fusion.3
  98.7 3.7 gather_fusion.1
  102.4 4.1 fusion.1
  107.9 2.8 fusion.9
  110.7 4.9 convolution_add_fusion.2
  115.9 2.3 fusion.59
  118.2 2.8 fusion.8
  121.0 4.9 convolution_add_fusion.3
  128.1 1.6 fusion.60
  131.0 100.8 %all-reduce.13.cloned.1.call-done = f32[64,16384]{1,0:T(8,128)} async-done(((f32[64,16384]{1,0:T(8,128)}), f32[64,16384]{1,0:T(8,128)}) %all-reduce.13.cloned.1.call-update) | async-done | bytes 4194320
  233.8 55.9 %reduce-scatter.3.cloned.1.call-done = f32[8,16384]{1,0:T(8,128)} async-done(((f32[64,16384]{1,0:T(8,128)}), f32[8,16384]{1,0:T(8,128)}) %reduce-scatter.3.cloned.1.call-update) | async-done | bytes 524304 | tf_op jit(solution)/shard_map/reduce_scatter | solution.py:108
  289.7 1.9 reshape.380
  292.3 209.0 %all-reduce.19.cloned.1.call-done = (f32[128,128]{0,1:T(8,128)}, f32[128,128]{0,1:T(8,128)}) async-done(((f32[128,128]{0,1:T(8,128)}, f32[128,128]{0,1:T(8,128)}), (f32[128,128]{0,1:T(8,128)}, f32[128,128]{0,1:T(8,128)})) %all-reduce.19.cloned.1.call-update) | async-done | bytes 131088 | tf_op jit(solution)/shard_map/psum | solution.py:79
  504.1 11.7 %cholesky.74 = f32[128,128]{1,0:T(8,128)S(1)} custom-call(f32[128,128]{1,0:T(8,128)S(1)} %get-tuple-element.24), custom_call_target="Cholesky" | custom-call | tf_op jit(solution)/shard_map/jit(cholesky)/cholesky | solution.py:28
  517.0 9.8 custom-call.14
  526.8 10.4 %all-reduce.23.cloned.1.call-done = (f32[128,1024]{0,1:T(8,128)}, f32[128,512]{0,1:T(8,128)}) async-done(((f32[128,1024]{0,1:T(8,128)}, f32[128,512]{0,1:T(8,128)}), (f32[128,1024]{0,1:T(8,128)}, f32[128,512]{0,1:T(8,128)})) %all-reduce.23.cloned.1.call-update) | async-done | bytes 786448 | tf_op jit(solution)/shard_map/psum | solution.py:110
  537.3 1.7 fusion.41
  540.8 11.7 %cholesky.85 = f32[128,128]{1,0:T(8,128)S(1)} custom-call(f32[128,128]{1,0:T(8,128)S(1)} %get-tuple-element.23), custom_call_target="Cholesky" | custom-call | tf_op jit(solution)/shard_map/jit(cholesky)/cholesky | solution.py:28
  553.9 9.8 custom-call.15
  565.6 3.8 collective-permute-start.16
  571.7 1.8 broadcast.338
  575.0 4.8 collective-permute-start.18
  580.4 1.4 collective-permute-done.17
  582.5 5.0 collective-permute-start.20
  589.7 5.0 collective-permute-start.22
  596.8 5.0 collective-permute-start.24
  604.0 5.0 collective-permute-start.26
  611.2 5.0 collective-permute-start.28
  619.2 6.6 collective-permute-done.29
  626.5 2.5 gather_fusion.5
  629.1 3.7 gather_fusion.4
  632.8 4.1 fusion.3
  638.3 2.8 fusion.11
  641.1 4.9 convolution_add_fusion
  646.5 2.3 fusion.63
  648.8 2.8 fusion.10
  651.6 4.9 convolution_add_fusion.1
  656.8 138.1 %all-reduce.17.cloned.1.call-done = (f32[128,128]{0,1:T(8,128)}, f32[128,128]{0,1:T(8,128)}) async-done(((f32[128,128]{0,1:T(8,128)}, f32[128,128]{0,1:T(8,128)}), (f32[128,128]{0,1:T(8,128)}, f32[128,128]{0,1:T(8,128)})) %all-reduce.17.cloned.1.call-update) | async-done | bytes 131088 | tf_op jit(solution)/shard_map/psum | solution.py:79
  796.7 11.7 %cholesky.96 = f32[128,128]{1,0:T(8,128)S(1)} custom-call(f32[128,128]{1,0:T(8,128)S(1)} %fusion.35), custom_call_target="Cholesky" | custom-call | tf_op jit(solution)/shard_map/jit(cholesky)/cholesky | solution.py:28
  809.1 104.8 %all-reduce.15.cloned.1.call-done = f32[64,16384]{1,0:T(8,128)} async-done(((f32[64,16384]{1,0:T(8,128)}), f32[64,16384]{1,0:T(8,128)}) %all-reduce.15.cloned.1.call-update) | async-done | bytes 4194320
  915.8 56.1 %reduce-scatter.5.cloned.1.call-done = f32[8,16384]{1,0:T(8,128)} async-done(((f32[64,16384]{1,0:T(8,128)}), f32[8,16384]{1,0:T(8,128)}) %reduce-scatter.5.cloned.1.call-update) | async-done | bytes 524304 | tf_op jit(solution)/shard_map/reduce_scatter | solution.py:108
  971.9 1.9 reshape.387
  974.5 9.8 custom-call.16
  984.5 11.7 %cholesky.107 = f32[128,128]{1,0:T(8,128)S(1)} custom-call(f32[128,128]{1,0:T(8,128)S(1)} %fusion.31), custom_call_target="Cholesky" | custom-call | tf_op jit(solution)/shard_map/jit(cholesky)/cholesky | solution.py:28
  997.5 10.0 custom-call.17
  1007.6 1.7 fusion.33
  (183 shorter events, 67.0 us)
Async XLA Ops:
  7.2 91.5 %all-gather.3.cloned.1.call-start = ((), (), s32[]{:S(2)}) async-start(), calls=%async_computation.4 | async-start | bytes 2359296 | tf_op jit(solution)/shard_map/all_gather | solution.py:98
  9.0 28.3 %copy-start.11 = (s32[1,1,1,64]{3,2,1,0:T(1,128)S(1)}, s32[1,1,1,64]{3,2,1,0:T(1,128)}, u32[]{:S(2)}) copy-start(s32[1,1,1,64]{3,2,1,0:T(1,128)} %param.20) | copy-start | bytes 772
  10.0 33.4 %copy-start.12 = (s32[1,1,1,64]{3,2,1,0:T(1,128)S(1)}, s32[1,1,1,64]{3,2,1,0:T(1,128)}, u32[]{:S(2)}) copy-start(s32[1,1,1,64]{3,2,1,0:T(1,128)} %param.19) | copy-start | bytes 772
  10.0 33.4 %collective-permute-start = (bf16[4,128,128]{2,1,0:T(8,128)(2,1)S(1)}, bf16[4,128,128]{2,1,0:T(8,128)(2,1)S(1)}, u32[]{:S(2)}, u32[]{:S(2)}) collective-permute-start(bf16[4,128,128]{2,1,0:T(8,128)(2,1)S(1)} %bitcast.221), channel_id=1, source_target_pairs={{0,16},{16,32},{32,48},{48,64},{64,80},{80,96},{96,112},{112,128},... | collective-permute-start | bytes 393224 | tf_op jit(solution)/shard_map/ppermute | solution.py:17
  12.2 31.5 %collective-permute-start.1 = (bf16[4,128,128]{2,1,0:T(8,128)(2,1)S(1)}, bf16[4,128,128]{2,1,0:T(8,128)(2,1)S(1)}, u32[]{:S(2)}, u32[]{:S(2)}) collective-permute-start(bf16[4,128,128]{2,1,0:T(8,128)(2,1)S(1)} %bitcast.222), channel_id=1, source_target_pairs={{0,240},{16,0},{32,16},{48,32},{64,48},{80,64},{96,80},{112,96},{1... | collective-permute-start | bytes 393224 | tf_op jit(solution)/shard_map/ppermute | solution.py:20
  17.3 9.8 all-to-all-start.1
  27.0 14.8 %all-to-all-start = ((s32[8,1,4]{2,1,0:T(1,128)}), s32[8,1,4]{2,1,0:T(1,128)S(1)}, u32[]{:S(2)}, u32[]{:S(2)}) async-start(s32[8,1,4]{2,1,0:T(1,128)} %copy.65), calls=%async_computation | async-start | bytes 8192 | tf_op jit(solution)/shard_map/all_to_all | solution.py:66
  35.2 196.6 %all-reduce.13.cloned.1.call-start = ((), (), s32[]{:S(2)}) async-start(), calls=%async_computation.8 | async-start | bytes 8388608
  43.4 7.2 collective-permute-start.2
  43.7 6.9 collective-permute-start.3
  50.6 7.1 collective-permute-start.4
  50.6 7.1 collective-permute-start.5
  57.8 7.1 collective-permute-start.6
  57.8 7.1 collective-permute-start.7
  64.9 8.0 collective-permute-start.8
  64.9 8.0 collective-permute-start.9
  72.9 8.2 collective-permute-start.10
  72.9 8.2 collective-permute-start.11
  81.1 7.1 collective-permute-start.12
  81.1 7.8 collective-permute-start.13
  88.2 7.1 collective-permute-start.14
  98.6 3.8 copy-start.9
  98.6 3.8 copy-start.10
  102.4 4.1 copy-start.1
  106.5 1.4 copy-start.2
  115.6 174.1 %reduce-scatter.3.cloned.1.call-start = ((), (), s32[]{:S(2)}) async-start(), calls=%async_computation.5 | async-start | bytes 4718592 | tf_op jit(solution)/shard_map/reduce_scatter | solution.py:108
  125.9 0.9 copy-start.5
  125.9 2.2 copy-start.4
  125.9 3.9 copy-start.13
  125.9 375.4 %all-reduce.19.cloned.1.call-start = ((), (), s32[]{:S(2)}) async-start(), calls=%async_computation.11 | async-start | bytes 262144 | tf_op jit(solution)/shard_map/psum | solution.py:79
  129.7 407.5 %all-reduce.23.cloned.1.call-start = ((), (), s32[]{:S(2)}) async-start(), calls=%async_computation.13 | async-start | bytes 1572864 | tf_op jit(solution)/shard_map/psum | solution.py:110
  291.7 337.4 %all-gather.5.cloned.1.call-start = ((), (), s32[]{:S(2)}) async-start(), calls=%async_computation.6 | async-start | bytes 2359296 | tf_op jit(solution)/shard_map/all_gather | solution.py:98
  537.3 26.4 %copy-start.7 = (f32[128,512]{0,1:T(8,128)S(1)}, f32[128,512]{0,1:T(8,128)}, u32[]{:S(2)}) copy-start(f32[128,512]{0,1:T(8,128)} %get-tuple-element.18) | copy-start | bytes 786436
  540.4 254.4 %all-reduce.17.cloned.1.call-start = ((), (), s32[]{:S(2)}) async-start(), calls=%async_computation.10 | async-start | bytes 262144 | tf_op jit(solution)/shard_map/psum | solution.py:79
  564.6 9.6 collective-permute-start.15
  565.6 9.4 collective-permute-start.16
  574.2 339.7 %all-reduce.15.cloned.1.call-start = ((), (), s32[]{:S(2)}) async-start(), calls=%async_computation.9 | async-start | bytes 8388608
  574.2 7.6 collective-permute-start.17
  575.0 7.5 collective-permute-start.18
  581.9 7.1 collective-permute-start.19
  582.5 7.1 collective-permute-start.20
  589.0 7.1 collective-permute-start.21
  589.7 7.1 collective-permute-start.22
  596.2 7.2 collective-permute-start.23
  596.8 7.2 collective-permute-start.24
  603.3 7.2 collective-permute-start.25
  604.0 7.2 collective-permute-start.26
  610.5 7.2 collective-permute-start.27
  611.2 7.4 collective-permute-start.28
  617.7 8.1 collective-permute-start.29
  632.8 4.1 copy-start
  636.9 1.4 copy-start.3
  646.0 325.9 %reduce-scatter.5.cloned.1.call-start = ((), (), s32[]{:S(2)}) async-start(), calls=%async_computation.7 | async-start | bytes 4718592 | tf_op jit(solution)/shard_map/reduce_scatter | solution.py:108
  656.5 351.0 %all-reduce.21.cloned.1.call-start = ((), (), s32[]{:S(2)}) async-start(), calls=%async_computation.12 | async-start | bytes 1572864 | tf_op jit(solution)/shard_map/psum | solution.py:110
  794.8 189.5 %copy-start.6 = (f32[128,128]{0,1:T(8,128)S(1)}, f32[128,128]{0,1:T(8,128)}, u32[]{:S(2)}) copy-start(f32[128,128]{0,1:T(8,128)} %get-tuple-element.12) | copy-start | bytes 196612
  1007.6 3.3 copy-start.8
Sparse Core Ops, SparseCore 0:
  10.4 41.2 all-gather.2
  115.8 116.0 all-reduce.12
  234.4 55.3 reduce-scatter.2
  295.2 206.0 all-reduce.18
  504.6 32.6 all-reduce.22
  540.6 38.2 all-gather.4
  585.0 209.8 all-reduce.16
  798.6 115.2 all-reduce.14
  916.6 55.3 reduce-scatter.4
  975.2 29.5 all-reduce.20
